TPU v7x, 128 devices: a whole 4x4x4 slice. The times are simulated.
128 devices in a mesh: left: 8 (over z, core), right: 16 (over y, x).
Axes of the slice: x: 4, y: 4, z: 4, core: 2. Of those that a mesh axis runs over, the one named last changes fastest.
Arguments:
- wavefunction: bfloat16 [10240, 10240], P('left', 'right'), may hold values from -6 to 6
- left_env: bfloat16 [8, 10240, 640], P(None, 'left'), may hold values from -0.25 to 0.25
- right_env: bfloat16 [8, 640, 10240], P(None, None, 'right'), may hold values from -0.25 to 0.25
- left_sizes: int32 [16], replicated, may hold values from 512 to 640, as said below
- right_sizes: int32 [16], replicated, may hold values from 512 to 640, as said below
- allowed: int32 [31], replicated, may hold values 0 or 1
- channel_shift: int32 [8], replicated, may hold values from -1 to 1, as said below
Outputs:
- evolved: bfloat16 [10240, 10240], P('left', 'right')
Inputs may be any that keep to these rules, and one draw needn't show every extreme that they name: `left_sizes`: multiples of 128; in every draw some left sector has exactly 640. `right_sizes`: multiples of 128; in every draw some right sector has exactly 640. `channel_shift`: each of -1, 0 and 1 occurs.
All inputs are finite; a program needn't handle non-finite values.
Results may differ from a plain program's by a relative error of at most 0.0054.
Values may be sent and summed in bfloat16 or wider, within the bound.
A program may use at most 192 MiB of HBM per device.

v0:
```python
import jax
import jax.numpy as jnp
from jax import lax
from jax.sharding import PartitionSpec as P

MAXS = 640
STEPS = 2


time_step = 0.5


def with_halo(block, sides, width):
    for axis, dim in sides:
        count = lax.axis_size(axis)
        forward = [(i, i + 1) for i in range(count - 1)]
        backward = [(target, source) for source, target in forward]
        low = lax.ppermute(
            lax.slice_in_dim(block, block.shape[dim] - width, None, axis=dim), axis, forward
        )
        high = lax.ppermute(lax.slice_in_dim(block, 0, width, axis=dim), axis, backward)
        block = jnp.concatenate([low, block, high], axis=dim)
    return block


def passed_along(shard, axis, by):
    peers = lax.axis_size(axis)
    pairs = [(i, i + by) for i in range(peers) if 0 <= i + by < peers]
    return lax.ppermute(shard, axis, pairs)


def body(wavefunction, left_env, right_env, left_sizes, right_sizes, allowed, channel_shift):
    local_rows = wavefunction.shape[0]
    local_sectors = local_rows // MAXS
    channels = left_env.shape[0]
    first_sector = lax.axis_index("left") * local_sectors
    column_sector = lax.axis_index("right")
    positions = jnp.arange(MAXS, dtype=jnp.int32)
    sector_rows = first_sector + jnp.arange(local_sectors, dtype=jnp.int32)
    row_sizes = lax.dynamic_slice_in_dim(left_sizes, first_sector, local_sectors)
    block_keep = allowed[sector_rows + column_sector] > 0
    row_keep = (positions[None, :] < row_sizes[:, None]) & block_keep[:, None]
    col_keep = positions < right_sizes[column_sector]
    keep_mask = (
        (row_keep[:, :, None] & col_keep[None, None, :])
        .reshape(local_rows, MAXS)
        .astype(jnp.float32)
    )
    current = (wavefunction.astype(jnp.float32) * keep_mask).astype(jnp.bfloat16)
    left_blocks = left_env.reshape(channels, local_sectors, MAXS, MAXS)
    source_index = jnp.arange(local_sectors, dtype=jnp.int32)[None, :] + 1 - channel_shift[:, None]
    shift_onehot = (channel_shift[None, :] == jnp.arange(3, dtype=jnp.int32)[:, None] - 1).astype(
        jnp.float32
    )
    widened_env = with_halo(right_env, (("right", 2),), MAXS)
    env_slots = widened_env.reshape(channels, MAXS, 3, MAXS)
    right_blocks = jnp.take_along_axis(env_slots, (1 - channel_shift)[:, None, None, None], axis=2)[
        :, :, 0, :
    ]
    for taylor_step in range(STEPS):
        extended = with_halo(current, (("left", 0),), MAXS)
        sector_slots = extended.reshape(local_sectors + 2, MAXS, MAXS)
        sources = sector_slots[source_index]
        partial_done = jnp.einsum(
            "wtik,wtkc->wtic", left_blocks, sources, preferred_element_type=jnp.float32
        )
        partial_done = partial_done.astype(jnp.bfloat16).reshape(channels, local_rows, MAXS)
        per_channel = jnp.einsum(
            "wrk,wkc->wrc", partial_done, right_blocks, preferred_element_type=jnp.float32
        )
        by_shift = jnp.einsum(
            "dw,wrc->drc", shift_onehot, per_channel, precision=lax.Precision.HIGHEST
        )
        from_above = passed_along(by_shift[2], "right", -1)
        from_below = passed_along(by_shift[0], "right", 1)
        applied = by_shift[1] + from_above + from_below
        current = ((current.astype(jnp.float32) - time_step * applied) * keep_mask).astype(
            jnp.bfloat16
        )
    return current


def solution(mesh):
    in_specs = (
        P("left", "right"),
        P(None, "left", None),
        P(None, None, "right"),
        P(),
        P(),
        P(),
        P(),
    )
    out_specs = P("left", "right")
    return jax.shard_map(body, mesh=mesh, in_specs=in_specs, out_specs=out_specs, check_vma=False)
```

profile of v0, /device:TPU:55, one launch (start us, length us, event | category | flops | bytes accessed | tf_op | source)
XLA Modules:
  0.0 558.3 jit_solution(9325994357488100116)
XLA Ops:
  0.0 0.0 copy-start
  0.0 0.0 copy-start.5
  0.0 9.6 %copy.13 = bf16[8,640,640]{1,2,0:T(8,128)(2,1)} copy(bf16[8,640,640]{2,1,0:T(8,128)(2,1)} %param.9) | data formatting | bytes 13107200 | tf_op args[2]
  9.7 2.6 collective-permute-start.3
  12.3 4.9 collective-permute-start.2
  17.2 0.0 copy-done.9
  17.2 0.1 dynamic_slice.6
  17.3 0.0 copy-done
  17.3 0.6 gather_fusion
  18.0 0.1 compare_and_fusion
  18.1 0.6 dynamic_slice.7
  18.7 0.6 iota_compare_fusion
  19.3 0.6 fusion.4
  19.9 0.0 copy-start.4
  19.9 1.2 copy-done.4
  21.1 0.1 fusion.32
  21.2 4.7 collective-permute-start
  25.9 1.9 collective-permute-start.1
  27.8 0.1 compare_select_fusion
  27.9 0.1 reshape.186
  28.0 7.1 %collective-permute-done = bf16[640,640]{1,0:T(8,128)(2,1)S(1)} collective-permute-done((bf16[640,640]{1,0:T(8,128)(2,1)S(1)}, bf16[640,640]{1,0:T(8,128)(2,1)S(1)}, u32[]{:S(2)}, u32[]{:S(2)}) %collective-permute-start) | collective-permute-done | bytes 819232 | tf_op jit(solution)/shard_map/ppermute | solution.py:18
  35.1 0.9 copy-done.7
  36.1 3.9 collective-permute-done.1
  39.9 2.2 pad_maximum_fusion.1
  42.1 6.9 %gather_fusion.1 = bf16[16,640,640]{2,1,0:T(8,128)(2,1)} fusion(bf16[4,640,640]{2,1,0:T(8,128)(2,1)S(1)} %bitcast.70, s32[1024]{0:T(1024)S(1)} %pad_clamp_fusion), kind=kCustom, calls=%fused_computation.1 | custom fusion | bytes 26214464 | tf_op jit(solution)/shard_map/gather | solution.py:63
  49.0 21.2 %convolution_convert_fusion.1 = bf16[8,2,640,640]{2,3,1,0:T(8,128)(2,1)} fusion(bf16[8,2,640,640]{3,2,1,0:T(8,128)(2,1)} %bitcast.79, bf16[8,2,640,640]{3,2,1,0:T(8,128)(2,1)} %bitcast.74), kind=kOutput, calls=%fused_computation.10 | convolution fusion | flops 8395161600 | bytes 39321600 | tf_op jit(solution)/shard_map/wtik,wtkc->wtic/dot_general | solution.py:64
  70.2 85.9 %collective-permute-done.3 = bf16[8,640,640]{1,2,0:T(8,128)(2,1)} collective-permute-done((bf16[8,640,640]{1,2,0:T(8,128)(2,1)}, bf16[8,640,640]{1,2,0:T(8,128)(2,1)}, u32[]{:S(2)}, u32[]{:S(2)}) %collective-permute-start.3) | collective-permute-done | bytes 6553632 | tf_op jit(solution)/shard_map/ppermute | solution.py:21
  156.1 0.9 collective-permute-done.2
  157.0 16.5 %pad_maximum_fusion = bf16[8,640,1920]{1,2,0:T(8,128)(2,1)} fusion(bf16[8,640,640]{1,2,0:T(8,128)(2,1)} %collective-permute-done.3, bf16[8,640,640]{1,2,0:T(8,128)(2,1)} %copy.13, bf16[8,640,640]{1,2,0:T(8,128)(2,1)} %collective-permute-done.2), kind=kLoop, calls=%fused_computation.8 | loop fusion | flops 58982400 | bytes 39321600 | tf_op jit(solution)/shard_map/concatenate | solution.py:22
  173.5 24.3 %copy.16 = bf16[8,640,3,640]{3,1,2,0:T(8,128)(2,1)} copy(bf16[8,640,3,640]{1,3,2,0:T(8,128)(2,1)} %bitcast.72) | data formatting | bytes 39321600 | tf_op jit(solution)/shard_map/reshape | solution.py:56
  197.7 10.7 %gather_fusion.3 = bf16[8,640,640]{2,1,0:T(8,128)(2,1)} fusion(bf16[8,640,3,640]{3,1,2,0:T(8,128)(2,1)} %copy.16, s32[8]{0:T(128)S(1)} %or_bitcast_fusion), kind=kCustom, calls=%fused_computation.3 | custom fusion | bytes 13107264 | tf_op jit(solution)/shard_map/jit(take_along_axis)/gather | solution.py:57
  208.4 21.8 %fusion.16 = f32[8,1280,640]{2,1,0:T(8,128)} fusion(bf16[8,1280,640]{2,1,0:T(8,128)(2,1)} %bitcast.81, bf16[8,640,640]{2,1,0:T(8,128)(2,1)} %gather_fusion.3, pred[8]{0:T(512)(128)(4,1)S(1)} %compare_and_fusion.1), kind=kOutput, calls=%fused_computation.35 | convolution fusion | flops 8391884800 | bytes 45875208 | tf_op jit(solution)/shard_map/wrk,wkc->wrc/dot_general | solution.py:68
  230.2 25.6 %fusion.2 = f32[3,1280,640]{2,0,1:T(4,128)} fusion(f32[8,1280,640]{2,1,0:T(8,128)} %fusion.16, s32[8]{0:T(128)S(1)} %copy-done.8, s32[3]{0:T(128)S(1)} %iota_add_fusion.1), kind=kOutput, calls=%fused_computation.6 | convolution fusion | flops 235929632 | bytes 36044844 | tf_op jit(solution)/shard_map/dw,wrc->drc/dot_general | solution.py:71
  255.8 21.6 %fusion.30 = (f32[1,1280,640]{2,0,1:T(1,128)S(1)}, f32[1,1280,640]{2,0,1:T(1,128)S(1)}, f32[1,1280,640]{2,0,1:T(1,128)S(1)}) fusion(f32[3,1280,640]{2,0,1:T(4,128)} %fusion.2), kind=kLoop, calls=%fused_computation.62 | loop fusion | bytes 19660800 | tf_op jit(solution)/shard_map/slice | solution.py:76
  277.4 0.0 copy-start.6
  277.4 0.2 copy.63
  277.6 0.2 copy.62
  277.8 2.1 collective-permute-start.4
  279.9 6.2 %collective-permute-start.5 = (f32[1280,640]{1,0:T(8,128)S(1)}, f32[1280,640]{1,0:T(8,128)S(1)}, u32[]{:S(2)}, u32[]{:S(2)}) collective-permute-start(f32[1280,640]{1,0:T(8,128)S(1)} %bitcast.75), channel_id=1, source_target_pairs={{0,1},{1,2},{2,3},{3,4},{4,5},{5,6},{6,7},{7,8},{8,9},{9,10},{10,1... | collective-permute-start | bytes 9830408 | tf_op jit(solution)/shard_map/ppermute | solution.py:29
  286.1 67.4 %collective-permute-done.4 = f32[1280,640]{1,0:T(8,128)S(1)} collective-permute-done((f32[1280,640]{1,0:T(8,128)S(1)}, f32[1280,640]{1,0:T(8,128)S(1)}, u32[]{:S(2)}, u32[]{:S(2)}) %collective-permute-start.4) | collective-permute-done | bytes 3276832 | tf_op jit(solution)/shard_map/ppermute | solution.py:29
  353.5 0.9 collective-permute-done.5
  354.4 0.0 copy-done.6
  354.4 1.7 fusion.5
  356.1 0.0 copy-start.2
  356.1 0.1 fusion.31
  356.3 6.2 %collective-permute-start.6 = (bf16[640,640]{1,0:T(8,128)(2,1)S(1)}, bf16[640,640]{1,0:T(8,128)(2,1)S(1)}, u32[]{:S(2)}, u32[]{:S(2)}) collective-permute-start(bf16[640,640]{1,0:T(8,128)(2,1)S(1)} %get-tuple-element.11), channel_id=1, source_target_pairs={{0,16},{16,32},{32,48},{48,64},{64,80},{80,96},{96,112},{1,17},{17... | collective-permute-start | bytes 2457608 | tf_op jit(solution)/shard_map/ppermute | solution.py:18
  362.5 1.9 collective-permute-start.7
  364.4 7.3 %collective-permute-done.6 = bf16[640,640]{1,0:T(8,128)(2,1)S(1)} collective-permute-done((bf16[640,640]{1,0:T(8,128)(2,1)S(1)}, bf16[640,640]{1,0:T(8,128)(2,1)S(1)}, u32[]{:S(2)}, u32[]{:S(2)}) %collective-permute-start.6) | collective-permute-done | bytes 819232 | tf_op jit(solution)/shard_map/ppermute | solution.py:18
  371.8 4.4 collective-permute-done.7
  376.2 0.3 pad_maximum_fusion.2
  376.5 6.9 %gather_fusion.2 = bf16[16,640,640]{2,1,0:T(8,128)(2,1)} fusion(bf16[4,640,640]{2,1,0:T(8,128)(2,1)S(1)} %bitcast.71, s32[1024]{0:T(1024)S(1)} %pad_clamp_fusion), kind=kCustom, calls=%fused_computation.2 | custom fusion | bytes 26214464 | tf_op jit(solution)/shard_map/gather | solution.py:63
  383.3 21.2 %convolution_convert_fusion = bf16[8,2,640,640]{2,3,1,0:T(8,128)(2,1)} fusion(bf16[8,2,640,640]{3,2,1,0:T(8,128)(2,1)} %bitcast.80, bf16[8,2,640,640]{3,2,1,0:T(8,128)(2,1)} %bitcast.73), kind=kOutput, calls=%fused_computation.9 | convolution fusion | flops 8395161600 | bytes 39321600 | tf_op jit(solution)/shard_map/wtik,wtkc->wtic/dot_general | solution.py:64
  404.6 21.7 %fusion.15 = f32[8,1280,640]{2,1,0:T(8,128)} fusion(bf16[8,1280,640]{2,1,0:T(8,128)(2,1)} %bitcast.82, bf16[8,640,640]{2,1,0:T(8,128)(2,1)} %gather_fusion.3, pred[8]{0:T(512)(128)(4,1)S(1)} %compare_and_fusion.1), kind=kOutput, calls=%fused_computation.34 | convolution fusion | flops 8391884800 | bytes 45875208 | tf_op jit(solution)/shard_map/wrk,wkc->wrc/dot_general | solution.py:68
  426.2 25.7 %fusion = f32[3,1280,640]{2,0,1:T(4,128)} fusion(f32[8,1280,640]{2,1,0:T(8,128)} %fusion.15, s32[8]{0:T(128)S(1)} %copy-done.8, s32[3]{0:T(128)S(1)} %iota_add_fusion.1), kind=kOutput, calls=%fused_computation.4 | convolution fusion | flops 235929632 | bytes 36044844 | tf_op jit(solution)/shard_map/dw,wrc->drc/dot_general | solution.py:71
  451.9 21.2 %fusion.29 = (f32[1,1280,640]{2,0,1:T(1,128)S(1)}, f32[1,1280,640]{2,0,1:T(1,128)S(1)}, f32[1,1280,640]{2,0,1:T(1,128)S(1)}) fusion(f32[3,1280,640]{2,0,1:T(4,128)} %fusion), kind=kLoop, calls=%fused_computation.61 | loop fusion | bytes 19660800 | tf_op jit(solution)/shard_map/slice | solution.py:76
  473.1 0.0 copy-start.3
  473.2 0.2 copy.61
  473.4 0.2 copy.60
  473.6 6.3 %collective-permute-start.9 = (f32[1280,640]{1,0:T(8,128)S(1)}, f32[1280,640]{1,0:T(8,128)S(1)}, u32[]{:S(2)}, u32[]{:S(2)}) collective-permute-start(f32[1280,640]{1,0:T(8,128)S(1)} %bitcast.78), channel_id=1, source_target_pairs={{0,1},{1,2},{2,3},{3,4},{4,5},{5,6},{6,7},{7,8},{8,9},{9,10},{10,1... | collective-permute-start | bytes 9830408 | tf_op jit(solution)/shard_map/ppermute | solution.py:29
  480.0 1.9 collective-permute-start.8
  481.9 67.6 %collective-permute-done.9 = f32[1280,640]{1,0:T(8,128)S(1)} collective-permute-done((f32[1280,640]{1,0:T(8,128)S(1)}, f32[1280,640]{1,0:T(8,128)S(1)}, u32[]{:S(2)}, u32[]{:S(2)}) %collective-permute-start.9) | collective-permute-done | bytes 3276832 | tf_op jit(solution)/shard_map/ppermute | solution.py:29
  549.4 6.2 %collective-permute-done.8 = f32[1280,640]{1,0:T(8,128)S(1)} collective-permute-done((f32[1280,640]{1,0:T(8,128)S(1)}, f32[1280,640]{1,0:T(8,128)S(1)}, u32[]{:S(2)}, u32[]{:S(2)}) %collective-permute-start.8) | collective-permute-done | bytes 3276832 | tf_op jit(solution)/shard_map/ppermute | solution.py:29
  555.7 2.5 fusion.6
  558.1 0.0 copy-done.1
  (22 shorter events, 0.1 us)
Async XLA Ops:
  0.0 17.3 %copy-start = (s32[31]{0:T(128)S(1)}, s32[31]{0:T(128)}, u32[]{:S(2)}) copy-start(s32[31]{0:T(128)} %param.12) | copy-start | bytes 376
  0.0 17.2 %copy-start.9 = (s32[16]{0:T(128)S(1)}, s32[16]{0:T(128)}, u32[]{:S(2)}) copy-start(s32[16]{0:T(128)} %param.10) | copy-start | bytes 196
  0.0 18.1 %copy-start.10 = (s32[16]{0:T(128)S(1)}, s32[16]{0:T(128)}, u32[]{:S(2)}) copy-start(s32[16]{0:T(128)} %param.11) | copy-start | bytes 196
  0.0 19.3 %copy-start.5 = (bf16[1280,640]{1,0:T(8,128)(2,1)S(1)}, bf16[1280,640]{1,0:T(8,128)(2,1)}, u32[]{:S(2)}) copy-start(bf16[1280,640]{1,0:T(8,128)(2,1)} %param.7) | copy-start | bytes 4915204
  9.7 18.1 %copy-start.8 = (s32[8]{0:T(128)S(1)}, s32[8]{0:T(128)}, u32[]{:S(2)}) copy-start(s32[8]{0:T(128)} %param.13) | copy-start | bytes 100
  9.7 146.4 %collective-permute-start.3 = (bf16[8,640,640]{1,2,0:T(8,128)(2,1)}, bf16[8,640,640]{1,2,0:T(8,128)(2,1)}, u32[]{:S(2)}, u32[]{:S(2)}) collective-permute-start(bf16[8,640,640]{1,2,0:T(8,128)(2,1)} %copy.13), channel_id=1, source_target_pairs={{1,0},{2,1},{3,2},{4,3},{5,4},{6,5},{7,6},{8,7},{9,8},{10,9},{11,1... | collective-permute-start | bytes 19660808 | tf_op jit(solution)/shard_map/ppermute | solution.py:21
  12.3 144.7 %collective-permute-start.2 = (bf16[8,640,640]{1,2,0:T(8,128)(2,1)}, bf16[8,640,640]{1,2,0:T(8,128)(2,1)}, u32[]{:S(2)}, u32[]{:S(2)}) collective-permute-start(bf16[8,640,640]{1,2,0:T(8,128)(2,1)} %copy.13), channel_id=1, source_target_pairs={{0,1},{1,2},{2,3},{3,4},{4,5},{5,6},{6,7},{7,8},{8,9},{9,10},{10,1... | collective-permute-start | bytes 19660808 | tf_op jit(solution)/shard_map/ppermute | solution.py:18
  19.9 1.2 copy-start.4
  21.2 13.9 %collective-permute-start = (bf16[640,640]{1,0:T(8,128)(2,1)S(1)}, bf16[640,640]{1,0:T(8,128)(2,1)S(1)}, u32[]{:S(2)}, u32[]{:S(2)}) collective-permute-start(bf16[640,640]{1,0:T(8,128)(2,1)S(1)} %get-tuple-element.13), channel_id=1, source_target_pairs={{0,16},{16,32},{32,48},{48,64},{64,80},{80,96},{96,112},{1,17},{17... | collective-permute-start | bytes 2457608 | tf_op jit(solution)/shard_map/ppermute | solution.py:18
  25.9 14.1 %collective-permute-start.1 = (bf16[640,640]{1,0:T(8,128)(2,1)S(1)}, bf16[640,640]{1,0:T(8,128)(2,1)}, u32[]{:S(2)}, u32[]{:S(2)}) collective-permute-start(bf16[640,640]{1,0:T(8,128)(2,1)S(1)} %get-tuple-element.14), channel_id=1, source_target_pairs={{16,0},{32,16},{48,32},{64,48},{80,64},{96,80},{112,96},{17,1},{33... | collective-permute-start | bytes 2457608 | tf_op jit(solution)/shard_map/ppermute | solution.py:21
  35.1 0.9 copy-start.7
  277.4 77.1 %copy-start.6 = (bf16[1280,640]{1,0:T(8,128)(2,1)S(1)}, bf16[1280,640]{1,0:T(8,128)(2,1)}, u32[]{:S(2)}) copy-start(bf16[1280,640]{1,0:T(8,128)(2,1)} %param.7) | copy-start | bytes 4915204
  277.8 75.7 %collective-permute-start.4 = (f32[1280,640]{1,0:T(8,128)S(1)}, f32[1280,640]{1,0:T(8,128)S(1)}, u32[]{:S(2)}, u32[]{:S(2)}) collective-permute-start(f32[1280,640]{1,0:T(8,128)S(1)} %bitcast.77), channel_id=1, source_target_pairs={{1,0},{2,1},{3,2},{4,3},{5,4},{6,5},{7,6},{8,7},{9,8},{10,9},{11,1... | collective-permute-start | bytes 9830408 | tf_op jit(solution)/shard_map/ppermute | solution.py:29
  279.9 74.5 %collective-permute-start.5 = (f32[1280,640]{1,0:T(8,128)S(1)}, f32[1280,640]{1,0:T(8,128)S(1)}, u32[]{:S(2)}, u32[]{:S(2)}) collective-permute-start(f32[1280,640]{1,0:T(8,128)S(1)} %bitcast.75), channel_id=1, source_target_pairs={{0,1},{1,2},{2,3},{3,4},{4,5},{5,6},{6,7},{7,8},{8,9},{9,10},{10,1... | collective-permute-start | bytes 9830408 | tf_op jit(solution)/shard_map/ppermute | solution.py:29
  356.1 20.0 %copy-start.2 = (bf16[1280,640]{1,0:T(8,128)(2,1)}, bf16[1280,640]{1,0:T(8,128)(2,1)S(1)}, u32[]{:S(2)}) copy-start(bf16[1280,640]{1,0:T(8,128)(2,1)S(1)} %fusion.5) | copy-start | bytes 4915204
  356.3 15.5 %collective-permute-start.6 = (bf16[640,640]{1,0:T(8,128)(2,1)S(1)}, bf16[640,640]{1,0:T(8,128)(2,1)S(1)}, u32[]{:S(2)}, u32[]{:S(2)}) collective-permute-start(bf16[640,640]{1,0:T(8,128)(2,1)S(1)} %get-tuple-element.11), channel_id=1, source_target_pairs={{0,16},{16,32},{32,48},{48,64},{64,80},{80,96},{96,112},{1,17},{17... | collective-permute-start | bytes 2457608 | tf_op jit(solution)/shard_map/ppermute | solution.py:18
  362.5 13.7 %collective-permute-start.7 = (bf16[640,640]{1,0:T(8,128)(2,1)S(1)}, bf16[640,640]{1,0:T(8,128)(2,1)S(1)}, u32[]{:S(2)}, u32[]{:S(2)}) collective-permute-start(bf16[640,640]{1,0:T(8,128)(2,1)S(1)} %get-tuple-element.12), channel_id=1, source_target_pairs={{16,0},{32,16},{48,32},{64,48},{80,64},{96,80},{112,96},{17,1},{33... | collective-permute-start | bytes 2457608 | tf_op jit(solution)/shard_map/ppermute | solution.py:21
  473.1 82.5 %copy-start.3 = (bf16[1280,640]{1,0:T(8,128)(2,1)S(1)}, bf16[1280,640]{1,0:T(8,128)(2,1)}, u32[]{:S(2)}) copy-start(bf16[1280,640]{1,0:T(8,128)(2,1)} %copy-done.2) | copy-start | bytes 4915204
  473.6 75.8 %collective-permute-start.9 = (f32[1280,640]{1,0:T(8,128)S(1)}, f32[1280,640]{1,0:T(8,128)S(1)}, u32[]{:S(2)}, u32[]{:S(2)}) collective-permute-start(f32[1280,640]{1,0:T(8,128)S(1)} %bitcast.78), channel_id=1, source_target_pairs={{0,1},{1,2},{2,3},{3,4},{4,5},{5,6},{6,7},{7,8},{8,9},{9,10},{10,1... | collective-permute-start | bytes 9830408 | tf_op jit(solution)/shard_map/ppermute | solution.py:29
  480.0 75.7 %collective-permute-start.8 = (f32[1280,640]{1,0:T(8,128)S(1)}, f32[1280,640]{1,0:T(8,128)S(1)}, u32[]{:S(2)}, u32[]{:S(2)}) collective-permute-start(f32[1280,640]{1,0:T(8,128)S(1)} %bitcast.76), channel_id=1, source_target_pairs={{1,0},{2,1},{3,2},{4,3},{5,4},{6,5},{7,6},{8,7},{9,8},{10,9},{11,1... | collective-permute-start | bytes 9830408 | tf_op jit(solution)/shard_map/ppermute | solution.py:29
  555.7 2.5 copy-start.1
where the time goes:
time: 567 us; the launch traced here: 558 us
  waiting for transfers between devices  252 us (44%)
  matrix products  137 us (24%)
  local copies, waits for them, and re-layouts  106 us (19%)
  starting transfers between devices  38.8 us (7%)
  other arithmetic  24.5 us (4%)
    ppermute x4, waiting for transfers between devices, passed_along(): return lax.ppermute(shard, axis, pairs)  142 us
    ppermute x3, waiting for transfers between devices, with_halo(): lax.ppermute(lax.slice_in_dim(block, 0, width, axis=dim), axis, backward)  94.2 us
    dot_general x2, matrix products, body(): jnp.einsum('dw,wrc->drc', shift_onehot, per_channel, precision=lax.Precis...  51.3 us
    dot_general x2, matrix products, body(): jnp.einsum('wrk,wkc->wrc', partial_done, right_blocks, preferred_element_...  43.5 us
    slice x2, local copies, waits for them, and re-layouts, body(): applied = by_shift[1] + from_above + from_below  42.8 us
    dot_general x2, matrix products, body(): jnp.einsum('wtik,wtkc->wtic', left_blocks, sources, preferred_element_typ...  42.4 us
    reshape x1, local copies, waits for them, and re-layouts, body(): env_slots = widened_env.reshape(channels, MAXS, 3, MAXS)  24.3 us
    concatenate x3, other arithmetic, with_halo(): block = jnp.concatenate([low, block, high], axis=dim)  19 us
  transfers between devices with their start and end apart: 10, of which 10 were waited for; matrix products, arithmetic and copies ran while one was open for 6% of the time, Pallas kernels for 0%

commit v1 on v0

v1 whole, which is shorter than its diff:
```python
import jax
import jax.numpy as jnp
from jax import lax
from jax.experimental import pallas as pl
from jax.experimental.pallas import tpu as pltpu
from jax.sharding import PartitionSpec as P

MAXS = 640
STEPS = 2
CHUNK = 256
ROW_TILE = 320
COMPUTE = True

time_step = 0.5

CHUNKS = tuple((at, min(CHUNK, MAXS - at)) for at in range(0, MAXS, CHUNK))
PARTS = len(CHUNKS)
MESH = pl.DeviceIdType.MESH


def kernel(left_sizes, right_sizes, allowed, channel_shift, wave, left_env, right_env, out, *scratch):
    scratch = list(scratch)
    lbuf, acc, half = scratch[:3]
    rbuf = scratch[3 : 3 + PARTS]
    flat = scratch[3 + PARTS : 3 + PARTS + 4 * PARTS]
    wave_sem, left_sem, right_sem, send_sem, recv_sem = scratch[3 + 5 * PARTS :]
    xs = [[flat[(2 * t + b) * PARTS : (2 * t + b + 1) * PARTS] for b in range(2)] for t in range(2)]
    channels = lbuf.shape[1]
    rows, cols = lax.axis_size("left"), lax.axis_size("right")
    me, col = lax.axis_index("left"), lax.axis_index("right")
    up, down = lax.rem(me + rows - 1, rows), lax.rem(me + 1, rows)
    before, after = lax.rem(col + cols - 1, cols), lax.rem(col + 1, cols)

    def fetch_wave(b, c):
        at, width = CHUNKS[c]
        return pltpu.make_async_copy(
            wave.at[pl.ds(b * MAXS, MAXS), pl.ds(at, width)], xs[0][b][c].at[1], wave_sem.at[b, c]
        )

    def fetch_left(b):
        return pltpu.make_async_copy(left_env.at[:, pl.ds(b * MAXS, MAXS), :], lbuf.at[b], left_sem.at[b])

    def fetch_right(c):
        at, width = CHUNKS[c]
        return pltpu.make_async_copy(right_env.at[:, pl.ds(at, width), :], rbuf[c], right_sem.at[c])

    for b in (1, 0):
        for c in range(PARTS):
            fetch_wave(b, c).start()
    fetch_left(0).start()
    for c in range(PARTS):
        fetch_right(c).start()
    fetch_left(1).start()

    barrier = pltpu.get_barrier_semaphore()
    for peer in ((me, before), (up, after), (down, before), (me, after)):
        pl.semaphore_signal(barrier, inc=1, device_id=peer, device_id_type=MESH)
    pl.semaphore_wait(barrier, 4)

    def copies(t, b, c):
        targets = ((2, (me if b == 0 else down, before)), (0, (up if b == 0 else me, after)))
        return [
            pltpu.make_async_remote_copy(
                src_ref=xs[t][b][c].at[1],
                dst_ref=xs[t][1 - b][c].at[slot],
                send_sem=send_sem.at[t, b, c, side],
                recv_sem=recv_sem.at[t, 1 - b, c, side],
                device_id=target,
                device_id_type=MESH,
            )
            for side, (slot, target) in enumerate(targets)
        ]

    def push(t, b, c):
        for copy in copies(t, b, c):
            copy.start()

    def arrive(t, b, c):
        for copy in copies(t, 1 - b, c):
            copy.wait_recv()
        no_after = col == cols - 1
        no_before = col == 0
        if b == 0:
            no_after = no_after | (me == 0)
        else:
            no_before = no_before | (me == rows - 1)
        for slot, missing in ((2, no_after), (0, no_before)):

            @pl.when(missing)
            def _():
                xs[t][b][c][slot] = jnp.zeros(xs[t][b][c].shape[1:], jnp.bfloat16)

    def keep(b, c):
        at, width = CHUNKS[c]
        sector = 2 * me + b
        row = lax.broadcasted_iota(jnp.int32, (MAXS, width), 0)
        column = lax.broadcasted_iota(jnp.int32, (MAXS, width), 1) + at
        row_limit = jnp.where(allowed[sector + col] == 1, left_sizes[sector], 0)
        return (row < row_limit) & (column < right_sizes[col])

    def absorb(t, b, c):
        width = CHUNKS[c][1]

        def channel(w, carry):
            source = xs[t][b][c][channel_shift[w] + 1]
            product = jnp.dot(lbuf[b, w], source, preferred_element_type=jnp.float32)
            half[:, pl.ds(pl.multiple_of(w * width, width), width)] = product.astype(jnp.bfloat16)
            return carry

        lax.fori_loop(0, channels, channel, 0)

        def tile(m, carry):
            span = pl.ds(pl.multiple_of(m * ROW_TILE, ROW_TILE), ROW_TILE)
            part = jnp.dot(
                half[span, : channels * width],
                rbuf[c][...].reshape(channels * width, MAXS),
                preferred_element_type=jnp.float32,
            )
            if c == 0:
                acc[span, :] = part
            else:
                acc[span, :] += part
            return carry

        lax.fori_loop(0, MAXS // ROW_TILE, tile, 0)

    def finish(t, b):
        for c, (at, width) in enumerate(CHUNKS):
            value = xs[t][b][c][1].astype(jnp.float32) - time_step * acc[:, at : at + width]
            value = jnp.where(keep(b, c), value, 0.0).astype(jnp.bfloat16)
            if t == 0:
                xs[1][b][c][1] = value
            else:
                out[b * MAXS : (b + 1) * MAXS, at : at + width] = value

    for b in (1, 0):
        for c in range(PARTS):
            fetch_wave(b, c).wait()
            value = xs[0][b][c][1].astype(jnp.float32)
            xs[0][b][c][1] = jnp.where(keep(b, c), value, 0.0).astype(jnp.bfloat16)
            if b == 1:
                push(0, 1, c)

    for t, b, follow in ((0, 0, (0, 0)), (0, 1, (1, 0)), (1, 1, (1, 1)), (1, 0, None)):
        if t == 0:
            fetch_left(b).wait()
        for c in range(PARTS):
            arrive(t, b, c)
            if follow is not None:
                push(*follow, c)
            if t == 0 and b == 0:
                fetch_right(c).wait()
            if COMPUTE:
                absorb(t, b, c)
        finish(t, b)

    for t in range(2):
        for b in range(2):
            for c in range(PARTS):
                for copy in copies(t, b, c):
                    copy.wait_send()


def body(wavefunction, left_env, right_env, left_sizes, right_sizes, allowed, channel_shift):
    channels = left_env.shape[0]
    scalars = pl.BlockSpec(memory_space=pltpu.SMEM)
    anywhere = pl.BlockSpec(memory_space=pl.ANY)
    return pl.pallas_call(
        kernel,
        out_shape=jax.ShapeDtypeStruct(wavefunction.shape, jnp.bfloat16),
        in_specs=[scalars] * 4 + [anywhere] * 3,
        out_specs=pl.BlockSpec(memory_space=pltpu.VMEM),
        scratch_shapes=[
            pltpu.VMEM((2, channels, MAXS, MAXS), jnp.bfloat16),
            pltpu.VMEM((MAXS, MAXS), jnp.float32),
            pltpu.VMEM((MAXS, channels * CHUNK), jnp.bfloat16),
            *[pltpu.VMEM((channels, width, MAXS), jnp.bfloat16) for _, width in CHUNKS],
            *[pltpu.VMEM((3, MAXS, width), jnp.bfloat16) for _ in range(4) for _, width in CHUNKS],
            pltpu.SemaphoreType.DMA((2, PARTS)),
            pltpu.SemaphoreType.DMA((2,)),
            pltpu.SemaphoreType.DMA((PARTS,)),
            pltpu.SemaphoreType.DMA((2, 2, PARTS, 2)),
            pltpu.SemaphoreType.DMA((2, 2, PARTS, 2)),
        ],
        compiler_params=pltpu.CompilerParams(
            collective_id=0, has_side_effects=True, vmem_limit_bytes=56 * 2**20
        ),
        name="taylor",
    )(left_sizes, right_sizes, allowed, channel_shift, wavefunction, left_env, right_env)


def solution(mesh):
    return jax.shard_map(
        body,
        mesh=mesh,
        in_specs=(P("left", "right"), P(None, "left", None), P(None, None, "right"), P(), P(), P(), P()),
        out_specs=P("left", "right"),
        check_vma=False,
    )
```

time: 567 us -> 92.8 us (0.16)
  the two profiles are of different devices: /device:TPU:55 before, /device:TPU:0 now
where the time goes in v1:
time: 92.8 us; the launch traced here: 92.6 us
  Pallas kernels  89.9 us (97%)
  local copies, waits for them, and re-layouts  2.74 us (3%)
    pallas_call x1, Pallas kernels, body(): pl.pallas_call(kernel, out_shape=jax.ShapeDtypeStruct(wavefunction.shape,...  89.9 us
    unnamed x1, local copies, waits for them, and re-layouts  2.74 us

profile of v1, /device:TPU:0, one launch (start us, length us, event | category | flops | bytes accessed | tf_op | source)
XLA Modules:
  0.0 92.6 jit_solution(4219651079367514178)
XLA Ops:
  0.0 89.9 %taylor.1 = bf16[1280,640]{1,0:T(8,128)(2,1)} custom-call(s32[16]{0:T(128)} %left_sizes.1, s32[16]{0:T(128)} %right_sizes.1, s32[31]{0:T(128)} %allowed.1, s32[8]{0:T(128)} %channel_shift.1, bf16[1280,640]{1,0:T(8,128)(2,1)} %wave.1, bf16[8,1280,640]{2,1,0:T(8,128)(2,1)} %left_env.1, bf16[8,640,640]{2,1,0:T(8,128)(2,1)} %right_env.1), custom_call_target="tpu_custom_call" | custom-call | tf_op jit(solution)/shard_map/taylor/pallas_call | solution.py:168
  89.9 2.7 %copy.9 = bf16[1280,640]{1,0:T(8,128)(2,1)} copy(bf16[1280,640]{1,0:T(8,128)(2,1)} %taylor.1) | data formatting | bytes 3276800
